TPU v7x, 512 devices: a whole 4x4x16 slice. The times are simulated.
512 devices in a mesh: chan: 16 (over z), inp: 32 (over x, y, core).
Axes of the slice: x: 4, y: 4, z: 16, core: 2. Of those that a mesh axis runs over, the one named last changes fastest.
Arguments:
- voltages: int32 [2, 1024, 16, 4096], P(None, 'chan', None, 'inp'), may hold values from -128 to 127
- fir_taps: float32 [4, 16], replicated, may hold values from -3 to 3
Outputs:
- visibilities: float32 [16, 2, 4096, 4096], P('chan', None, 'inp')
All inputs are finite; a program needn't handle non-finite values.
Results may differ from a plain program's by a relative error of at most 0.0036.
Values may be sent and summed in bfloat16 or wider, within the bound.
A program may use at most 128 MiB of HBM per device.

v0:
```python
import math

import jax
import jax.numpy as jnp
from jax import lax
from jax.sharding import PartitionSpec as P

volt_scale = 1.0 / 256.0


def passed_along(x, axis, by):
    count = lax.axis_size(axis)
    pairs = [(i, i + by) for i in range(count) if 0 <= i + by < count]
    return lax.ppermute(x, axis, pairs)


def dft_tables(count):
    index = jnp.arange(count, dtype=jnp.int32)
    phase = index[:, None] * index[None, :] % count
    angle = phase.astype(jnp.float32) * (2.0 * math.pi / count)
    return (jnp.cos(angle), jnp.sin(angle))


def transform(filtered, count):
    cosine, sine = dft_tables(count)
    real_in = filtered[0]
    imag_in = filtered[1]
    high = lax.Precision.HIGHEST
    real_out = jnp.einsum("cn,snb->csb", cosine, real_in, precision=high) + jnp.einsum(
        "cn,snb->csb", sine, imag_in, precision=high
    )
    imag_out = jnp.einsum("cn,snb->csb", cosine, imag_in, precision=high) - jnp.einsum(
        "cn,snb->csb", sine, real_in, precision=high
    )
    return (jnp.stack([real_out, imag_out], 1) * volt_scale).astype(jnp.bfloat16)


def body(voltages, fir_taps):
    frames = voltages.shape[1]
    chans = voltages.shape[2]
    tap_count = fir_taps.shape[0]
    early_rim = passed_along(voltages[:, frames - (tap_count - 1) :], "chan", 1)
    extended = jnp.concatenate([early_rim, voltages], 1).astype(jnp.float32)
    filtered = (
        fir_taps[0][None, None, :, None] * extended[:, tap_count - 1 : tap_count - 1 + frames]
    )
    for tap_index in range(1, tap_count):
        begin = tap_count - 1 - tap_index
        filtered = (
            filtered
            + fir_taps[tap_index][None, None, :, None] * extended[:, begin : begin + frames]
        )
    spectra = transform(filtered, chans)
    turned = lax.all_to_all(spectra, "chan", split_axis=0, concat_axis=2, tiled=True)
    norm_factor = 1.0 / turned.shape[2]
    piece = lax.all_gather(turned, "inp", axis=3, tiled=True)
    rotated = jnp.concatenate([-piece[:, 1:2], piece[:, 0:1]], axis=1)
    real_part = jnp.einsum("cpsi,cpsj->cij", turned, piece, preferred_element_type=jnp.float32)
    imag_part = jnp.einsum("cpsi,cpsj->cij", turned, rotated, preferred_element_type=jnp.float32)
    return jnp.stack([real_part, imag_part], 1) * norm_factor


def solution(mesh):
    placed = (P(None, "chan", None, "inp"), P())
    return jax.shard_map(
        body, mesh=mesh, in_specs=placed, out_specs=P("chan", None, "inp", None), check_vma=False
    )
```

profile of v0, /device:TPU:1, one launch (start us, length us, event | category | flops | bytes accessed | tf_op | source)
XLA Modules:
  0.0 183.6 jit_solution(8837996353936311876)
XLA Ops:
  6.5 0.0 all-gather.2.cloned.1.call-start
  6.5 0.8 slice.40
  7.3 4.3 %collective-permute-start = (s32[2,3,16,128]{3,2,1,0:T(8,128)S(1)}, s32[2,3,16,128]{3,2,1,0:T(8,128)S(1)}, u32[]{:S(2)}, u32[]{:S(2)}) collective-permute-start(s32[2,3,16,128]{3,2,1,0:T(8,128)S(1)} %slice.40), channel_id=1, source_target_pairs={{0,32},{32,64},{64,96},{96,128},{128,160},{160,192},{192,224},{224... | collective-permute-start | bytes 147464 | tf_op jit(solution)/shard_map/ppermute | solution.py:14
  11.7 0.8 slice_bitcast_fusion.9
  12.5 0.3 collective-permute-done
  12.9 1.3 add_convert_fusion
  14.2 0.3 fusion.11
  14.5 0.6 fusion.15
  15.1 0.6 fusion.16
  15.7 0.6 fusion.10
  16.3 0.6 fusion.9
  17.0 0.1 fusion.14
  17.1 0.1 copy.7
  17.2 38.5 %all_to_all.18 = bf16[16,2,64,128]{3,2,1,0:T(8,128)(2,1)S(1)} all-to-all(bf16[16,2,64,128]{3,2,1,0:T(8,128)(2,1)S(1)} %copy.7), channel_id=1, replica_groups=mesh['chan'=16,'inp'=32] {'chan'}, dimensions={0} | all-to-all | bytes 1048576 | tf_op jit(solution)/shard_map/all_to_all | solution.py:54
  55.7 0.8 copy.8
  56.6 0.0 all-gather.2.cloned.1.call-update
  56.6 0.0 copy-start
  56.6 98.2 %all-gather.2.cloned.1.call-done = bf16[1,2,1024,4096]{3,2,1,0:T(8,128)(2,1)} async-done(((bf16[1,2,1024,128]{3,2,1,0:T(8,128)(2,1)}), bf16[1,2,1024,4096]{3,2,1,0:T(8,128)(2,1)}) %all-gather.2.cloned.1.call-update) | async-done | bytes 16777232 | tf_op jit(solution)/shard_map/all_gather | solution.py:56
  154.9 0.0 slice-start
  154.9 0.0 slice-start.1
  154.9 10.6 %slice_negate_fusion = (bf16[1,1,1024,4096]{3,2,1,0:T(8,128)(2,1)S(1)}, bf16[1,1,1024,4096]{3,2,1,0:T(8,128)(2,1)}) fusion(bf16[1,2,1024,4096]{3,2,1,0:T(8,128)(2,1)} %all-gather.2.cloned.1.call-done), kind=kLoop, calls=%fused_computation.6 | loop fusion | flops 4194304 | bytes 33554432 | tf_op jit(solution)/shard_map/neg | solution.py:57
  165.5 0.0 copy-done
  165.5 0.0 slice-start.2
  165.5 0.0 slice-start.3
  165.5 6.5 %fusion.8 = f32[1,1,128,4096]{3,2,1,0:T(8,128)S(1)} fusion(bf16[2,1024,128]{2,1,0:T(8,128)(2,1)S(1)} %bitcast.60, bf16[1,1,1024,4096]{3,2,1,0:T(8,128)(2,1)} %get-tuple-element.6, bf16[1,1,1024,4096]{3,2,1,0:T(8,128)(2,1)S(1)} %get-tuple-element.5), kind=kOutput, calls=%fused_computation.8 | convolution fusion | flops 2155872256 | bytes 19398656 | tf_op jit(solution)/shard_map/cpsi,cpsj->cij/dot_general | solution.py:59
  172.0 0.0 slice-done
  172.0 0.0 slice-done.1
  172.0 0.0 slice-done.2
  172.0 0.0 slice-done.3
  172.0 2.4 %fusion.5 = f32[1,1,128,4096]{3,2,1,0:T(8,128)S(1)} fusion(bf16[2,1024,128]{2,1,0:T(8,128)(2,1)S(1)} %bitcast.61, bf16[1,2,1024,4096]{3,2,1,0:T(8,128)(2,1)S(1)} %bitcast.58), kind=kOutput, calls=%fused_computation.7 | convolution fusion | flops 2147483648 | bytes 19398656 | tf_op jit(solution)/shard_map/cpsi,cpsj->cij/dot_general | solution.py:58
  174.4 2.3 %maximum_multiply_fusion = f32[1,2,128,4096]{3,2,1,0:T(8,128)} fusion(f32[1,1,128,4096]{3,2,1,0:T(8,128)S(1)} %fusion.8, f32[1,1,128,4096]{3,2,1,0:T(8,128)S(1)} %fusion.5), kind=kLoop, calls=%fused_computation.9 | loop fusion | flops 2097152 | bytes 8388608 | tf_op jit(solution)/shard_map/mul | solution.py:60
  (1 shorter events, 0.0 us)
Async XLA Ops:
  6.5 148.3 %all-gather.2.cloned.1.call-start = ((), (), s32[]{:S(2)}) async-start(), calls=%async_computation.1 | async-start | bytes 17301504 | tf_op jit(solution)/shard_map/all_gather | solution.py:56
  7.3 5.5 %collective-permute-start = (s32[2,3,16,128]{3,2,1,0:T(8,128)S(1)}, s32[2,3,16,128]{3,2,1,0:T(8,128)S(1)}, u32[]{:S(2)}, u32[]{:S(2)}) collective-permute-start(s32[2,3,16,128]{3,2,1,0:T(8,128)S(1)} %slice.40), channel_id=1, source_target_pairs={{0,32},{32,64},{64,96},{96,128},{128,160},{160,192},{192,224},{224... | collective-permute-start | bytes 147464 | tf_op jit(solution)/shard_map/ppermute | solution.py:14
  56.6 108.8 %copy-start = (bf16[16,2,64,128]{3,2,0,1:T(8,128)(2,1)S(1)}, bf16[16,2,64,128]{3,2,0,1:T(8,128)(2,1)}, u32[]{:S(2)}) copy-start(bf16[16,2,64,128]{3,2,0,1:T(8,128)(2,1)} %copy.8) | copy-start | bytes 1572868
  154.9 17.1 %slice-start = ((s8[16777216]{0:T(1024)(128)(4,1)}), s8[4194304]{0:T(1024)(128)(4,1)S(1)}, s32[]{:S(2)}) async-start(s8[16777216]{0:T(1024)(128)(4,1)} %bitcast.57), calls=%async_computation.2 | async-start | bytes 8388608
  154.9 17.1 %slice-start.1 = ((s8[16777216]{0:T(1024)(128)(4,1)}), s8[4194304]{0:T(1024)(128)(4,1)S(1)}, s32[]{:S(2)}) async-start(s8[16777216]{0:T(1024)(128)(4,1)} %bitcast.57), calls=%async_computation.3 | async-start | bytes 8388608
  165.5 6.5 %slice-start.2 = ((s8[16777216]{0:T(1024)(128)(4,1)}), s8[4194304]{0:T(1024)(128)(4,1)S(1)}, s32[]{:S(2)}) async-start(s8[16777216]{0:T(1024)(128)(4,1)} %bitcast.57), calls=%async_computation.4 | async-start | bytes 8388608
  165.5 6.5 %slice-start.3 = ((s8[16777216]{0:T(1024)(128)(4,1)}), s8[4194304]{0:T(1024)(128)(4,1)S(1)}, s32[]{:S(2)}) async-start(s8[16777216]{0:T(1024)(128)(4,1)} %bitcast.57), calls=%async_computation.5 | async-start | bytes 8388608
Sparse Core Ops, SparseCore 0:
  56.7 98.0 all-gather.1
where the time goes:
time: 184 us
  waiting for transfers between devices  98.6 us (54%)
  blocking collectives  38.5 us (21%)
  other arithmetic  14.6 us (8%)
  between operations  13.5 us (7%)
  matrix products  11.3 us (6%)
  starting transfers between devices  4.35 us (2%)
  local copies, waits for them, and re-layouts  2.63 us (1%)
    all_gather x1, waiting for transfers between devices, body(): piece = lax.all_gather(turned, 'inp', axis=3, tiled=True)  98.2 us
    all_to_all x1, blocking collectives, body(): lax.all_to_all(spectra, 'chan', split_axis=0, concat_axis=2, tiled=True)  38.5 us
    neg x1, other arithmetic, body(): rotated = jnp.concatenate([-piece[:, 1:2], piece[:, 0:1]], axis=1)  10.6 us
    dot_general x1, matrix products, body(): jnp.einsum('cpsi,cpsj->cij', turned, rotated, preferred_element_type=jnp....  6.5 us
    ppermute x1, starting transfers between devices, passed_along(): return lax.ppermute(x, axis, pairs)  4.35 us
  transfers between devices with their start and end apart: 2, of which 2 were waited for; matrix products, arithmetic and copies ran while one was open for 0% of the time, Pallas kernels for 0%

commit v1 on v0

--- a/solution.py
+++ b/solution.py
@@ -1,8 +1,11 @@
+import functools
 import math
 
 import jax
 import jax.numpy as jnp
 from jax import lax
+from jax.experimental import pallas as pl
+from jax.experimental.pallas import tpu as pltpu
 from jax.sharding import PartitionSpec as P
 
 volt_scale = 1.0 / 256.0
@@ -33,6 +36,203 @@
         "cn,snb->csb", sine, real_in, precision=high
     )
     return (jnp.stack([real_out, imag_out], 1) * volt_scale).astype(jnp.bfloat16)
+
+
+grid_x = 4
+grid_y = 4
+MESH = pl.DeviceIdType.MESH
+
+
+def exchange_kernel(
+    zs, spectra, out, store,
+    sem_a, sem_b, sem_c, sem_d, sem_d2, sem_e, sem_e2, sem_p, send_a, send_g, send_p,
+):
+    rounds = zs // 2
+    chips = grid_x * grid_y
+    span = spectra.shape[2]
+    lanes = spectra.shape[3]
+    z = lax.axis_index("chan")
+    inp = lax.axis_index("inp")
+    core = lax.rem(inp, 2)
+    chip = lax.div(inp, 2)
+    y = lax.rem(chip, grid_y)
+    x = lax.div(chip, grid_y)
+
+    def chip_of(part, u, v):
+        first, second = (u, v) if part == 0 else (v, u)
+        return lax.rem(first + 4, 4) * grid_y + lax.rem(second + 4, 4)
+
+    here = ((x, y), (y, x))
+    barrier = pltpu.get_barrier_semaphore()
+
+    def greet_z(step, carry):
+        pl.semaphore_signal(
+            barrier, inc=1, device_id={"chan": lax.rem(z + step, zs)}, device_id_type=MESH
+        )
+        return carry
+
+    lax.fori_loop(1, zs, greet_z, 0)
+    for du, dv in ((1, 0), (-1, 0), (0, 1), (0, -1)):
+        pl.semaphore_signal(
+            barrier, inc=1,
+            device_id={"inp": chip_of(0, x + du, y + dv) * 2 + core}, device_id_type=MESH,
+        )
+    pl.semaphore_signal(barrier, inc=1, device_id={"inp": chip * 2 + 1 - core}, device_id_type=MESH)
+
+    out[...] = jnp.zeros_like(out)
+    pl.semaphore_wait(barrier, zs + 4)
+
+    def z_slot(source):
+        rows = pl.ds(pl.multiple_of(lax.rem(source, 2) * span, span), span)
+        return store.at[lax.div(source, 2), core, :, chip, rows]
+
+    own_copy = pltpu.make_async_copy(spectra.at[z], z_slot(z), sem_a.at[z])
+    own_copy.start()
+
+    def turn(step, carry):
+        away = lax.div(step, 2) + 1
+        target = lax.rem(z + (1 - 2 * lax.rem(step, 2)) * away + zs, zs)
+        pltpu.make_async_remote_copy(
+            src_ref=spectra.at[target], dst_ref=z_slot(z), send_sem=send_a, recv_sem=sem_a.at[z],
+            device_id={"chan": target}, device_id_type=MESH,
+        ).start()
+        return carry
+
+    lax.fori_loop(0, zs - 1, turn, 0)
+
+    def pair_of(turn_index):
+        off = lax.div(turn_index + 1, 2) * (2 * lax.rem(turn_index, 2) - 1)
+        return lax.rem(lax.div(z, 2) + off + rounds, rounds)
+
+    def arrive(sem, ref):
+        pltpu.make_async_copy(ref, ref, sem).wait()
+
+    def pass_on(t, pair, part, source, target, sem):
+        block = store.at[pair, core, part, source]
+        pltpu.make_async_remote_copy(
+            src_ref=block, dst_ref=block, send_sem=send_g.at[t], recv_sem=sem.at[t],
+            device_id={"inp": target * 2 + core}, device_id_type=MESH,
+        ).start()
+
+    def stage(t, action):
+        @pl.when(jnp.logical_and(t >= 0, t < rounds))
+        def _():
+            action(t, pair_of(t))
+
+    def step_a(t, pair):
+        for source in (2 * pair, 2 * pair + 1):
+            arrive(sem_a.at[source], z_slot(source))
+        for part in (0, 1):
+            u, v = here[part]
+            for way in (1, -1):
+                pass_on(t, pair, part, chip, chip_of(part, u + way, v), sem_b)
+
+    def step_b(t, pair):
+        arrive(sem_b.at[t], store.at[pair, core, :, pl.ds(0, 2)])
+        for part in (0, 1):
+            u, v = here[part]
+            way = 1 - 2 * lax.rem(t + part, 2)
+            pass_on(t, pair, part, chip_of(part, u - way, v), chip_of(part, u + way, v), sem_c)
+        for shift in (0, 1, -1):
+            for part in (0, 1):
+                u, v = here[part]
+                for way in (1, -1):
+                    pass_on(t, pair, part, chip_of(part, u + shift, v), chip_of(part, u, v + way), sem_d)
+
+    def step_c(t, pair):
+        arrive(sem_c.at[t], store.at[pair, core, :, 0])
+        for part in (0, 1):
+            u, v = here[part]
+            for way in (1, -1):
+                pass_on(t, pair, part, chip_of(part, u + 2, v), chip_of(part, u, v + way), sem_d2)
+
+    def across(t, pair, shift, sem):
+        for part in (0, 1):
+            u, v = here[part]
+            way = 1 - 2 * lax.rem(t + part + u + shift + 4, 2)
+            pass_on(t, pair, part, chip_of(part, u + shift, v - way), chip_of(part, u, v + way), sem)
+
+    def step_d(t, pair):
+        arrive(sem_d.at[t], store.at[pair, core, :, pl.ds(0, 6)])
+        for shift in (0, 1, -1):
+            across(t, pair, shift, sem_e)
+
+    def step_d2(t, pair):
+        arrive(sem_d2.at[t], store.at[pair, core, :, pl.ds(0, 2)])
+        across(t, pair, 2, sem_e2)
+
+    def step_e(t, pair):
+        arrive(sem_e.at[t], store.at[pair, core, :, pl.ds(0, 3)])
+        arrive(sem_e2.at[t], store.at[pair, core, :, 0])
+        block = store.at[pair, core]
+        pltpu.make_async_remote_copy(
+            src_ref=block, dst_ref=block, send_sem=send_p.at[t], recv_sem=sem_p.at[t],
+            device_id={"inp": chip * 2 + 1 - core}, device_id_type=MESH,
+        ).start()
+
+    def correlate(t, pair):
+        arrive(sem_p.at[t], store.at[pair, 1 - core])
+        real = store[pair, core, 0, chip].astype(jnp.float32).T
+        imag = store[pair, core, 1, chip].astype(jnp.float32).T
+        rows = jnp.concatenate(
+            [jnp.concatenate([real, imag], 1), jnp.concatenate([imag, -real], 1)], 0
+        ).astype(jnp.bfloat16)
+
+        def one_chip(n, carry):
+            block = jnp.concatenate(
+                [
+                    jnp.concatenate([store[pair, 0, part, n], store[pair, 1, part, n]], 1)
+                    for part in (0, 1)
+                ],
+                0,
+            )
+            product = jnp.dot(rows, block, preferred_element_type=jnp.float32)
+            columns = pl.ds(pl.multiple_of(n * (2 * lanes), 2 * lanes), 2 * lanes)
+            out[0, 0, :, columns] += product[:lanes]
+            out[0, 1, :, columns] += product[lanes:]
+            return carry
+
+        lax.fori_loop(0, chips, one_chip, 0)
+
+    def iteration(it, carry):
+        stage(it, step_a)
+        stage(it - 1, step_b)
+        stage(it - 2, step_c)
+        stage(it - 2, step_d)
+        stage(it - 3, step_d2)
+        stage(it - 4, step_e)
+        stage(it - 5, correlate)
+        return carry
+
+    lax.fori_loop(0, rounds + 5, iteration, 0)
+
+    arrive(send_a, spectra.at[pl.ds(0, zs - 1)])
+
+    def drain(t, carry):
+        arrive(send_g.at[t], store.at[0, 0, :, pl.ds(0, 15)])
+        arrive(send_p.at[t], store.at[0, 0])
+        return carry
+
+    lax.fori_loop(0, rounds, drain, 0)
+
+
+def exchange(spectra):
+    zs, parts, span, lanes = spectra.shape
+    rounds = zs // 2
+    chips = grid_x * grid_y
+    dma = pltpu.SemaphoreType.DMA
+    return pl.pallas_call(
+        functools.partial(exchange_kernel, zs),
+        out_shape=jax.ShapeDtypeStruct((1, 2, lanes, 2 * chips * lanes), jnp.float32),
+        in_specs=[pl.BlockSpec(memory_space=pltpu.VMEM)],
+        out_specs=pl.BlockSpec(memory_space=pltpu.VMEM),
+        scratch_shapes=[pltpu.VMEM((rounds, 2, 2, chips, 2 * span, lanes), jnp.bfloat16), dma((zs,))]
+        + [dma((rounds,))] * 7
+        + [dma, dma((rounds,)), dma((rounds,))],
+        compiler_params=pltpu.CompilerParams(
+            collective_id=0, has_side_effects=True, vmem_limit_bytes=40 * 1024 * 1024
+        ),
+    )(spectra)
 
 
 def body(voltages, fir_taps):
@@ -51,13 +251,8 @@
             + fir_taps[tap_index][None, None, :, None] * extended[:, begin : begin + frames]
         )
     spectra = transform(filtered, chans)
-    turned = lax.all_to_all(spectra, "chan", split_axis=0, concat_axis=2, tiled=True)
-    norm_factor = 1.0 / turned.shape[2]
-    piece = lax.all_gather(turned, "inp", axis=3, tiled=True)
-    rotated = jnp.concatenate([-piece[:, 1:2], piece[:, 0:1]], axis=1)
-    real_part = jnp.einsum("cpsi,cpsj->cij", turned, piece, preferred_element_type=jnp.float32)
-    imag_part = jnp.einsum("cpsi,cpsj->cij", turned, rotated, preferred_element_type=jnp.float32)
-    return jnp.stack([real_part, imag_part], 1) * norm_factor
+    norm_factor = 1.0 / (frames * lax.axis_size("chan"))
+    return exchange(spectra) * norm_factor
 
 
 def solution(mesh):

time: 184 us -> 99.3 us (0.54)
  waiting for transfers between devices: 98.6 us -> 0.32 us
  Pallas kernels: 0 us -> 85.5 us
  blocking collectives: 38.5 us -> 0 us
  between operations: 13.5 us -> 0.07 us
  other arithmetic: 14.6 us -> 4.79 us
  matrix products: 11.3 us -> 2.44 us
    all_gather x1 -> x0, waiting for transfers between devices: 98.2 us -> none  [body(): piece = lax.all_gather(turned, 'inp', axis=3, tiled=True)]
    pallas_call x0 -> x1, Pallas kernels: none -> 85.5 us  [exchange(): pl.pallas_call(functools.partial(exchange_kernel, zs), out_shape=jax.Shap...]
    all_to_all x1 -> x0, blocking collectives: 38.5 us -> none  [body(): lax.all_to_all(spectra, 'chan', split_axis=0, concat_axis=2, tiled=True)]
    neg x1 -> x0, other arithmetic: 10.6 us -> none  [body(): rotated = jnp.concatenate([-piece[:, 1:2], piece[:, 0:1]], axis=1)]
    dot_general x2 -> x0, matrix products: 8.87 us -> none  [the longest x1 6.5 us: body(): jnp.einsum('cpsi,cpsj->cij', turned, rotated, preferred_element_type=jnp....]
  transfers between devices with their start and end apart: 2 -> 1, of which waited for: 2 -> 1; matrix products, arithmetic and copies ran while one was open for 0% -> 1% of each run, Pallas kernels for 0% -> 0%
where the time goes in v1:
time: 99.3 us; the launch traced here: 99.1 us
  Pallas kernels  85.5 us (86%)
  other arithmetic  4.79 us (5%)
  starting transfers between devices  4.35 us (4%)
  matrix products  2.44 us (2%)
  local copies, waits for them, and re-layouts  1.64 us (2%)
    pallas_call x1, Pallas kernels, exchange(): pl.pallas_call(functools.partial(exchange_kernel, zs), out_shape=jax.Shap...  85.5 us
    ppermute x1, starting transfers between devices, passed_along(): return lax.ppermute(x, axis, pairs)  4.35 us
    mul x1, other arithmetic, body(): return exchange(spectra) * norm_factor  2.48 us
  transfers between devices with their start and end apart: 1, of which 1 were waited for; matrix products, arithmetic and copies ran while one was open for 1% of the time, Pallas kernels for 0%

profile of v1, /device:TPU:1, one launch (start us, length us, event | category | flops | bytes accessed | tf_op | source)
XLA Modules:
  0.0 99.1 jit_solution(573010699265550565)
XLA Ops:
  0.0 0.8 slice.34
  0.8 4.3 %collective-permute-start = (s32[2,3,16,128]{3,2,1,0:T(8,128)S(1)}, s32[2,3,16,128]{3,2,1,0:T(8,128)S(1)}, u32[]{:S(2)}, u32[]{:S(2)}) collective-permute-start(s32[2,3,16,128]{3,2,1,0:T(8,128)S(1)} %slice.34), channel_id=1, source_target_pairs={{0,32},{32,64},{64,96},{96,128},{128,160},{160,192},{192,224},{224... | collective-permute-start | bytes 147464 | tf_op jit(solution)/shard_map/ppermute | solution.py:17
  5.2 0.8 slice_bitcast_fusion.9
  6.0 0.3 collective-permute-done
  6.3 1.3 %add_convert_fusion = f32[2,67,16,128]{3,2,1,0:T(8,128)S(1)} fusion(s32[2,64,16,128]{3,2,1,0:T(8,128)} %param.2, s32[2,3,16,128]{3,2,1,0:T(8,128)S(1)} %collective-permute-done), kind=kLoop, calls=%fused_computation.1 | loop fusion | flops 548864 | bytes 2195456 | tf_op jit(solution)/shard_map/convert_element_type | solution.py:243
  7.6 0.3 fusion
  7.9 0.6 fusion.8
  8.6 0.6 fusion.6
  9.2 0.6 fusion.9
  9.8 0.6 fusion.7
  10.4 0.6 fusion.4
  11.0 0.1 fusion.3.spectra
  11.1 85.5 %shard_map.28 = f32[1,2,128,4096]{3,2,1,0:T(8,128)S(1)} custom-call(bf16[16,2,64,128]{3,2,1,0:T(8,128)(2,1)S(1)} %fusion.3.spectra), custom_call_target="tpu_custom_call" | custom-call | tf_op jit(solution)/shard_map/pallas_call | solution.py:224
  96.6 2.5 %broadcast_multiply_fusion = f32[1,2,128,4096]{3,2,1,0:T(8,128)} fusion(f32[1,2,128,4096]{3,2,1,0:T(8,128)S(1)} %shard_map.28), kind=kLoop, calls=%fused_computation | loop fusion | flops 1048576 | bytes 8388608 | tf_op jit(solution)/shard_map/mul | solution.py:255
Async XLA Ops:
  0.8 5.5 %collective-permute-start = (s32[2,3,16,128]{3,2,1,0:T(8,128)S(1)}, s32[2,3,16,128]{3,2,1,0:T(8,128)S(1)}, u32[]{:S(2)}, u32[]{:S(2)}) collective-permute-start(s32[2,3,16,128]{3,2,1,0:T(8,128)S(1)} %slice.34), channel_id=1, source_target_pairs={{0,32},{32,64},{64,96},{96,128},{128,160},{160,192},{192,224},{224... | collective-permute-start | bytes 147464 | tf_op jit(solution)/shard_map/ppermute | solution.py:17

commit v2 on v0

v2 whole, which is shorter than its diff:
```python
import functools
import math

import jax
import jax.numpy as jnp
import numpy as np
from jax import lax
from jax.experimental import pallas as pl
from jax.experimental.pallas import tpu as pltpu
from jax.sharding import PartitionSpec as P


def passed_along(x, axis, by):
    count = lax.axis_size(axis)
    pairs = [(i, i + by) for i in range(count) if 0 <= i + by < count]
    return lax.ppermute(x, axis, pairs)


def dft_rows(count, tap_count):
    index = np.arange(count)
    angle = (index[:, None] * index[None, :] % count) * (2.0 * math.pi / count)
    cosine, sine = np.cos(angle), np.sin(angle)
    real_out = np.concatenate([cosine, sine], 1)
    imag_out = np.concatenate([-sine, cosine], 1)
    rows = np.stack([real_out, imag_out], 1).reshape(2 * count, 2 * count)
    return np.tile(rows, (1, tap_count)).astype(np.float32)


volt_scale = 1.0 / 256.0
LAGS = (2, 4, 6, 6, 8, 12)
grid_x = 4
grid_y = 4
MESH = pl.DeviceIdType.MESH


def exchange_kernel(
    zs, volts, rim, taps, table, out, store, rows, frames, stage_f32, spectra,
    sem_a, sem_b, sem_c, sem_d, sem_f, sem_g, sem_p, send_a, send_b, send_r, send_p,
):
    chips = grid_x * grid_y
    span = spectra.shape[2]
    lanes = spectra.shape[3]
    early = rim.shape[1]
    reach = early + 1
    z = lax.axis_index("chan")
    inp = lax.axis_index("inp")
    core = lax.rem(inp, 2)
    chip = lax.div(inp, 2)
    y = lax.rem(chip, grid_y)
    x = lax.div(chip, grid_y)
    here = ((x, y), (y, x))

    def wrap(index):
        return lax.rem(index + 4, 4)

    def device_of(part, u, v):
        first, second = (u, v) if part == 0 else (v, u)
        return (wrap(first) * grid_y + wrap(second)) * 2 + core

    partner = chip * 2 + 1 - core

    barrier = pltpu.get_barrier_semaphore()

    def greet_z(step, carry):
        pl.semaphore_signal(
            barrier, inc=1, device_id={"chan": lax.rem(z + step, zs)}, device_id_type=MESH
        )
        return carry

    lax.fori_loop(1, zs, greet_z, 0)
    for du, dv in ((1, 0), (-1, 0), (0, 1), (0, -1)):
        pl.semaphore_signal(
            barrier, inc=1, device_id={"inp": device_of(0, x + du, y + dv)}, device_id_type=MESH
        )
    pl.semaphore_signal(barrier, inc=1, device_id={"inp": partner}, device_id_type=MESH)

    for part in (0, 1):
        samples = pl.ds(part * zs, zs)
        frames[0:early, samples] = rim[part].astype(jnp.float32).astype(jnp.bfloat16)
        frames[early:, samples] = volts[part].astype(jnp.float32).astype(jnp.bfloat16)
    later_first = [taps[k : k + 1] for k in range(early, -1, -1) for part in (0, 1)]
    weights = table[...] * jnp.concatenate(later_first, 1)
    coarse = weights.astype(jnp.bfloat16)
    rest = weights - coarse.astype(jnp.float32)
    middle = rest.astype(jnp.bfloat16)
    fine = (rest - middle.astype(jnp.float32)).astype(jnp.bfloat16)
    pieces = jnp.concatenate([coarse, middle, fine], 0)
    outs = 2 * zs

    def channelize(s, carry):
        pair = [frames[pl.ds(first, reach)].reshape(reach * outs, lanes) for first in (s, s + span // 2)]
        product = jnp.dot(
            pieces, jnp.concatenate(pair, 1), preferred_element_type=jnp.float32
        )
        total = (product[:outs] + (product[outs : 2 * outs] + product[2 * outs :])) * volt_scale
        for n, first in enumerate((s, s + span // 2)):
            stage_f32[pl.ds(first, outs, stride=span), :] = total[:, n * lanes : (n + 1) * lanes]
        return carry

    lax.fori_loop(0, span // 2, channelize, 0, unroll=2)
    spectra[...] = stage_f32[...].reshape(spectra.shape).astype(jnp.bfloat16)
    out[...] = jnp.zeros_like(out)
    pl.semaphore_wait(barrier, zs + 4)

    def own_block(source, part):
        u, v = here[part]
        return store.at[source, core, part, v, u]

    for part in (0, 1):
        pltpu.make_async_copy(spectra.at[z, part], own_block(z, part), sem_a.at[z]).start()

    def offset_of(turn):
        return lax.div(turn + 1, 2) * (2 * lax.rem(turn, 2) - 1)

    def corner_turn(turn, carry):
        target = lax.rem(z + offset_of(turn) + zs, zs)
        for part in (0, 1):
            pltpu.make_async_remote_copy(
                src_ref=spectra.at[target, part], dst_ref=own_block(z, part),
                send_sem=send_a, recv_sem=sem_a.at[z],
                device_id={"chan": target}, device_id_type=MESH,
            ).start()
        return carry

    lax.fori_loop(1, zs, corner_turn, 0)

    def source_of(turn):
        return lax.rem(z + offset_of(turn) + zs, zs)

    def arrive(sem, ref):
        pltpu.make_async_copy(ref, ref, sem).wait()

    def give(ref, target, send, recv):
        pltpu.make_async_remote_copy(
            src_ref=ref, dst_ref=ref, send_sem=send, recv_sem=recv,
            device_id={"inp": target}, device_id_type=MESH,
        ).start()

    def stage(t, action):
        @pl.when(jnp.logical_and(t >= 0, t < zs))
        def _():
            action(t, source_of(t))

    def way_of(t, part):
        return 1 - 2 * lax.rem(t + part, 2)

    def step_a(t, k):
        arrive(sem_a.at[k], store.at[k, core, :, 0, 0])
        for part in (0, 1):
            u, v = here[part]
            for side in (1, -1):
                give(store.at[k, core, part, v, u], device_of(part, u + side, v), send_b.at[t], sem_b.at[t])

    def step_b(t, k):
        arrive(sem_b.at[t], store.at[k, core, :, 0, pl.ds(0, 2)])
        for part in (0, 1):
            u, v = here[part]
            way = way_of(t, part)
            give(
                store.at[k, core, part, v, wrap(u - way)], device_of(part, u + way, v),
                send_b.at[t], sem_c.at[t],
            )

    def give_row(t, k, part, row, way, recv):
        u, v = here[part]
        give(store.at[k, core, part, wrap(row)], device_of(part, u, v + way), send_r.at[t], recv)

    def share_row(t, k, part, row):
        give(store.at[k, core, part, wrap(row)], partner, send_p.at[t], sem_p.at[t])

    def step_c(t, k):
        arrive(sem_c.at[t], store.at[k, core, :, 0, 0])
        for part in (0, 1):
            give_row(t, k, part, here[part][1], way_of(t, part), sem_d.at[t])

    def step_f(t, k):
        for part in (0, 1):
            give_row(t, k, part, here[part][1], -way_of(t, part), sem_f.at[t])

    def step_d(t, k):
        arrive(sem_d.at[t], store.at[k, core, :, 0])
        for part in (0, 1):
            v = here[part][1]
            way = way_of(t, part)
            give_row(t, k, part, v - way, way, sem_g.at[t])
        for part in (0, 1):
            v = here[part][1]
            share_row(t, k, part, v)
            share_row(t, k, part, v - way_of(t, part))

    def step_e(t, k):
        arrive(sem_f.at[t], store.at[k, core, :, 0])
        arrive(sem_g.at[t], store.at[k, core, :, 0])
        for part in (0, 1):
            v = here[part][1]
            share_row(t, k, part, v + way_of(t, part))
            share_row(t, k, part, v + 2)

    def correlate(t, quarter):
        ks = [source_of(t + step) for step in range(4)]

        @pl.when(quarter == 0)
        def _():
            for step, k in enumerate(ks):
                arrive(sem_p.at[t + step], store.at[k, 1 - core])
            depth = 4 * span
            mine = []
            for part in (0, 1):
                u, v = here[part]
                both = jnp.concatenate([store[k, core, part, v, u] for k in ks], 0)
                mine.append(both.astype(jnp.float32).T)
            real, imag = mine
            rows[:lanes, :depth] = real.astype(jnp.bfloat16)
            rows[:lanes, depth:] = imag.astype(jnp.bfloat16)
            rows[lanes:, :depth] = imag.astype(jnp.bfloat16)
            rows[lanes:, depth:] = (-real).astype(jnp.bfloat16)

        left = rows[...]
        for second in range(grid_y):
            block = jnp.concatenate(
                [
                    jnp.concatenate([store[k, c, 0, second, quarter] for c in (0, 1)], 1) for k in ks
                ]
                + [
                    jnp.concatenate([store[k, c, 1, quarter, second] for c in (0, 1)], 1) for k in ks
                ],
                0,
            )
            product = jnp.dot(left, block, preferred_element_type=jnp.float32)
            begin = (quarter * grid_y + second) * (2 * lanes)
            columns = pl.ds(pl.multiple_of(begin, 2 * lanes), 2 * lanes)
            out[0, 0, :, columns] += product[:lanes]
            out[0, 1, :, columns] += product[lanes:]

    def iteration(it, carry):
        stage(it, step_a)
        stage(it - LAGS[0], step_b)
        stage(it - LAGS[1], step_c)
        stage(it - LAGS[3], step_f)
        late = it - LAGS[5]

        @pl.when(jnp.logical_and(late >= 0, late < zs))
        def _():
            quarter = lax.rem(late, 4)
            correlate(late - quarter, quarter)

        stage(it - LAGS[2], step_d)
        stage(it - LAGS[4], step_e)
        return carry

    lax.fori_loop(0, zs + LAGS[5], iteration, 0)

    arrive(send_a, spectra.at[pl.ds(0, zs - 1)])

    def drain(t, carry):
        arrive(send_b.at[t], store.at[0, 0, :, 0, pl.ds(0, 3)])
        arrive(send_r.at[t], store.at[0, 0, :, pl.ds(0, 3)])
        arrive(send_p.at[t], store.at[0, 0])
        return carry

    lax.fori_loop(0, zs, drain, 0)


def exchange(volts, rim, taps):
    parts, span, zs, lanes = volts.shape
    early = rim.shape[1]
    chips = grid_x * grid_y
    table = dft_rows(zs, early + 1)
    dma = pltpu.SemaphoreType.DMA
    return pl.pallas_call(
        functools.partial(exchange_kernel, zs),
        out_shape=jax.ShapeDtypeStruct((1, 2, lanes, 2 * chips * lanes), jnp.float32),
        in_specs=[pl.BlockSpec(memory_space=pltpu.VMEM)] * 4,
        out_specs=pl.BlockSpec(memory_space=pltpu.VMEM),
        scratch_shapes=[
            pltpu.VMEM((zs, 2, 2, grid_y, grid_x, span, lanes), jnp.bfloat16),
            pltpu.VMEM((2 * lanes, 8 * span), jnp.bfloat16),
            pltpu.VMEM((early + span, 2 * zs, lanes), jnp.bfloat16),
            pltpu.VMEM((2 * zs * span, lanes), jnp.float32),
            pltpu.VMEM((zs, 2, span, lanes), jnp.bfloat16),
        ]
        + [dma((zs,))] * 7
        + [dma]
        + [dma((zs,))] * 3,
        compiler_params=pltpu.CompilerParams(
            collective_id=0, has_side_effects=True, vmem_limit_bytes=40 * 1024 * 1024
        ),
    )(volts, rim, taps, table)


def body(voltages, fir_taps):
    frames = voltages.shape[1]
    tap_count = fir_taps.shape[0]
    rim = passed_along(voltages[:, frames - (tap_count - 1) :], "chan", 1)
    norm_factor = 1.0 / (frames * lax.axis_size("chan"))
    return exchange(voltages, rim, fir_taps) * norm_factor


def solution(mesh):
    placed = (P(None, "chan", None, "inp"), P())
    return jax.shard_map(
        body, mesh=mesh, in_specs=placed, out_specs=P("chan", None, "inp", None), check_vma=False
    )
```

time: 184 us -> 87.5 us (0.48)
  waiting for transfers between devices: 98.6 us -> 1.16 us
  Pallas kernels: 0 us -> 75.9 us
  blocking collectives: 38.5 us -> 0 us
  between operations: 13.5 us -> 0.02 us
  other arithmetic: 14.6 us -> 2.43 us
  matrix products: 11.3 us -> 0 us
    all_gather x1 -> x0, waiting for transfers between devices: 98.2 us -> none  [body(): piece = lax.all_gather(turned, 'inp', axis=3, tiled=True)]
    pallas_call x0 -> x1, Pallas kernels: none -> 75.9 us  [exchange(): pl.pallas_call(functools.partial(exchange_kernel, zs), out_shape=jax.Shap...]
    all_to_all x1 -> x0, blocking collectives: 38.5 us -> none  [body(): lax.all_to_all(spectra, 'chan', split_axis=0, concat_axis=2, tiled=True)]
    dot_general x6 -> x0, matrix products: 11.3 us -> none  [the longest x1 6.5 us: body(): jnp.einsum('cpsi,cpsj->cij', turned, rotated, preferred_element_type=jnp....]
    neg x1 -> x0, other arithmetic: 10.6 us -> none  [body(): rotated = jnp.concatenate([-piece[:, 1:2], piece[:, 0:1]], axis=1)]
    unnamed x10 -> x6, local copies, waits for them, and re-layouts: 0.02 us -> 2.62 us
  transfers between devices with their start and end apart: 2 -> 1, of which waited for: 2 -> 1; matrix products, arithmetic and copies ran while one was open for 0% -> 0% of each run, Pallas kernels for 0% -> 0%
where the time goes in v2:
time: 87.5 us; the launch traced here: 87.2 us
  Pallas kernels  75.9 us (87%)
  starting transfers between devices  4.35 us (5%)
  local copies, waits for them, and re-layouts  3.42 us (4%)
  other arithmetic  2.43 us (3%)
  waiting for transfers between devices  1.16 us (1%)
    pallas_call x1, Pallas kernels, exchange(): pl.pallas_call(functools.partial(exchange_kernel, zs), out_shape=jax.Shap...  75.9 us
    ppermute x1, starting transfers between devices, passed_along(): return lax.ppermute(x, axis, pairs)  4.35 us
    unnamed x6, local copies, waits for them, and re-layouts  2.62 us
    mul x1, other arithmetic, body(): return exchange(voltages, rim, fir_taps) * norm_factor  2.43 us
  transfers between devices with their start and end apart: 1, of which 1 were waited for; matrix products, arithmetic and copies ran while one was open for 0% of the time, Pallas kernels for 0%

profile of v2, /device:TPU:1, one launch (start us, length us, event | category | flops | bytes accessed | tf_op | source)
XLA Modules:
  0.0 87.2 jit_solution(13563402839351786342)
XLA Ops:
  0.0 0.8 slice.3
  0.8 4.3 %collective-permute-start = (s32[2,3,16,128]{3,2,1,0:T(8,128)S(1)}, s32[2,3,16,128]{3,2,1,0:T(8,128)S(1)}, u32[]{:S(2)}, u32[]{:S(2)}) collective-permute-start(s32[2,3,16,128]{3,2,1,0:T(8,128)S(1)} %slice.3), channel_id=1, source_target_pairs={{0,32},{32,64},{64,96},{96,128},{128,160},{160,192},{192,224},{224... | collective-permute-start | bytes 147464 | tf_op jit(solution)/shard_map/ppermute | solution.py:16
  5.2 1.2 %collective-permute-done.rim = s32[2,3,16,128]{3,2,1,0:T(8,128)S(1)} collective-permute-done((s32[2,3,16,128]{3,2,1,0:T(8,128)S(1)}, s32[2,3,16,128]{3,2,1,0:T(8,128)S(1)}, u32[]{:S(2)}, u32[]{:S(2)}) %collective-permute-start) | collective-permute-done | bytes 49184 | tf_op jit(solution)/shard_map/ppermute | solution.py:16
  6.3 0.0 copy-start
  6.3 1.2 %copy-done = s32[2,64,16,128]{3,2,1,0:T(8,128)S(1)} copy-done((s32[2,64,16,128]{3,2,1,0:T(8,128)S(1)}, s32[2,64,16,128]{3,2,1,0:T(8,128)}, u32[]{:S(2)}) %copy-start) | copy-done | bytes 1048600
  7.5 0.0 copy-start.1
  7.5 0.7 copy-done.1
  8.3 0.0 copy-start.2
  8.3 0.7 copy-done.2
  8.9 75.9 %shard_map.37 = f32[1,2,128,4096]{3,2,1,0:T(8,128)S(1)} custom-call(s32[2,64,16,128]{3,2,1,0:T(8,128)S(1)} %copy-done, s32[2,3,16,128]{3,2,1,0:T(8,128)S(1)} %collective-permute-done.rim, f32[4,16]{1,0:T(4,128)S(1)} %copy-done.2, f32[32,128]{1,0:T(8,128)S(1)} %copy-done.1), custom_call_target="tpu_custom_call" | custom-call | tf_op jit(solution)/shard_map/pallas_call | solution.py:270
  84.8 2.4 %broadcast_multiply_fusion = f32[1,2,128,4096]{3,2,1,0:T(8,128)} fusion(f32[1,2,128,4096]{3,2,1,0:T(8,128)S(1)} %shard_map.37), kind=kLoop, calls=%fused_computation | loop fusion | flops 1048576 | bytes 8388608 | tf_op jit(solution)/shard_map/mul | solution.py:296
Async XLA Ops:
  0.8 5.5 %collective-permute-start = (s32[2,3,16,128]{3,2,1,0:T(8,128)S(1)}, s32[2,3,16,128]{3,2,1,0:T(8,128)S(1)}, u32[]{:S(2)}, u32[]{:S(2)}) collective-permute-start(s32[2,3,16,128]{3,2,1,0:T(8,128)S(1)} %slice.3), channel_id=1, source_target_pairs={{0,32},{32,64},{64,96},{96,128},{128,160},{160,192},{192,224},{224... | collective-permute-start | bytes 147464 | tf_op jit(solution)/shard_map/ppermute | solution.py:16
  6.3 1.2 %copy-start = (s32[2,64,16,128]{3,2,1,0:T(8,128)S(1)}, s32[2,64,16,128]{3,2,1,0:T(8,128)}, u32[]{:S(2)}) copy-start(s32[2,64,16,128]{3,2,1,0:T(8,128)} %volts.1) | copy-start | bytes 3145732
  7.5 0.7 copy-start.1
  8.3 0.7 copy-start.2

commit v3 on v2

--- a/solution.py
+++ b/solution.py
@@ -3,45 +3,43 @@
 
 import jax
 import jax.numpy as jnp
-import numpy as np
 from jax import lax
 from jax.experimental import pallas as pl
 from jax.experimental.pallas import tpu as pltpu
 from jax.sharding import PartitionSpec as P
 
 
-def passed_along(x, axis, by):
-    count = lax.axis_size(axis)
-    pairs = [(i, i + by) for i in range(count) if 0 <= i + by < count]
-    return lax.ppermute(x, axis, pairs)
-
-
-def dft_rows(count, tap_count):
-    index = np.arange(count)
-    angle = (index[:, None] * index[None, :] % count) * (2.0 * math.pi / count)
-    cosine, sine = np.cos(angle), np.sin(angle)
-    real_out = np.concatenate([cosine, sine], 1)
-    imag_out = np.concatenate([-sine, cosine], 1)
-    rows = np.stack([real_out, imag_out], 1).reshape(2 * count, 2 * count)
-    return np.tile(rows, (1, tap_count)).astype(np.float32)
-
-
 volt_scale = 1.0 / 256.0
 LAGS = (2, 4, 6, 6, 8, 12)
+DIRECT = 2
 grid_x = 4
 grid_y = 4
 MESH = pl.DeviceIdType.MESH
 
 
+def dft_entries(count, tap_count):
+    shape = (2 * count, 2 * count * tap_count)
+    row = lax.broadcasted_iota(jnp.int32, shape, 0)
+    column = lax.broadcasted_iota(jnp.int32, shape, 1)
+    channel, imag_out = row // 2, row % 2
+    imag_in, sample = (column // count) % 2, column % count
+    phase = (channel * sample + (imag_out - imag_in + 4) * (count // 4)) % count
+    entries = jnp.zeros(shape, jnp.float32)
+    for step in range(count):
+        entries = jnp.where(phase == step, math.cos(2.0 * math.pi * step / count), entries)
+    return entries
+
+
 def exchange_kernel(
-    zs, volts, rim, taps, table, out, store, rows, frames, stage_f32, spectra,
+    zs, volts_far, taps_far, out_far,
+    out, store, rows, frames, stage_f32, spectra, volts, taps, rim, sem_load, sem_rim, sem_out,
     sem_a, sem_b, sem_c, sem_d, sem_f, sem_g, sem_p, send_a, send_b, send_r, send_p,
 ):
     chips = grid_x * grid_y
     span = spectra.shape[2]
     lanes = spectra.shape[3]
-    early = rim.shape[1]
-    reach = early + 1
+    reach = taps.shape[0]
+    early = reach - 1
     z = lax.axis_index("chan")
     inp = lax.axis_index("inp")
     core = lax.rem(inp, 2)
@@ -59,6 +57,13 @@
 
     partner = chip * 2 + 1 - core
 
+    loads = (
+        pltpu.make_async_copy(volts_far, volts, sem_load.at[0]),
+        pltpu.make_async_copy(taps_far, taps, sem_load.at[1]),
+    )
+    for copy in loads:
+        copy.start()
+
     barrier = pltpu.get_barrier_semaphore()
 
     def greet_z(step, carry):
@@ -68,18 +73,20 @@
         return carry
 
     lax.fori_loop(1, zs, greet_z, 0)
-    for du, dv in ((1, 0), (-1, 0), (0, 1), (0, -1)):
+    for du, dv in ((1, 0), (-1, 0), (2, 0), (0, 1), (0, -1), (0, 2)):
         pl.semaphore_signal(
             barrier, inc=1, device_id={"inp": device_of(0, x + du, y + dv)}, device_id_type=MESH
         )
     pl.semaphore_signal(barrier, inc=1, device_id={"inp": partner}, device_id_type=MESH)
 
+    for copy in loads:
+        copy.wait()
     for part in (0, 1):
-        samples = pl.ds(part * zs, zs)
-        frames[0:early, samples] = rim[part].astype(jnp.float32).astype(jnp.bfloat16)
-        frames[early:, samples] = volts[part].astype(jnp.float32).astype(jnp.bfloat16)
+        frames[early:, part * zs : (part + 1) * zs] = (
+            volts[part].astype(jnp.float32).astype(jnp.bfloat16)
+        )
     later_first = [taps[k : k + 1] for k in range(early, -1, -1) for part in (0, 1)]
-    weights = table[...] * jnp.concatenate(later_first, 1)
+    weights = dft_entries(zs, reach) * jnp.concatenate(later_first, 1)
     coarse = weights.astype(jnp.bfloat16)
     rest = weights - coarse.astype(jnp.float32)
     middle = rest.astype(jnp.bfloat16)
@@ -87,20 +94,41 @@
     pieces = jnp.concatenate([coarse, middle, fine], 0)
     outs = 2 * zs
 
-    def channelize(s, carry):
-        pair = [frames[pl.ds(first, reach)].reshape(reach * outs, lanes) for first in (s, s + span // 2)]
-        product = jnp.dot(
-            pieces, jnp.concatenate(pair, 1), preferred_element_type=jnp.float32
-        )
+    def channelize(*spots):
+        columns = [frames[pl.ds(s, reach)].reshape(reach * outs, lanes) for s in spots]
+        product = jnp.dot(pieces, jnp.concatenate(columns, 1), preferred_element_type=jnp.float32)
         total = (product[:outs] + (product[outs : 2 * outs] + product[2 * outs :])) * volt_scale
-        for n, first in enumerate((s, s + span // 2)):
-            stage_f32[pl.ds(first, outs, stride=span), :] = total[:, n * lanes : (n + 1) * lanes]
-        return carry
-
-    lax.fori_loop(0, span // 2, channelize, 0, unroll=2)
-    spectra[...] = stage_f32[...].reshape(spectra.shape).astype(jnp.bfloat16)
+        for n, s in enumerate(spots):
+            stage_f32[pl.ds(s, outs, stride=span), :] = total[:, n * lanes : (n + 1) * lanes]
+
+    def channelize_pair(step, carry):
+        channelize(early + step, early + step + half)
+        return carry
+
+    half = (span - early) // 2
+    lax.fori_loop(0, half, channelize_pair, 0, unroll=2)
+    if early + 2 * half < span:
+        channelize(span - 1)
+    lead = min(16, span // 2)
+    staged = stage_f32[: outs * span].reshape(spectra.shape)
+    spectra[:, :, lead:] = staged[:, :, lead:].astype(jnp.bfloat16)
     out[...] = jnp.zeros_like(out)
-    pl.semaphore_wait(barrier, zs + 4)
+    pl.semaphore_wait(barrier, zs + 6)
+
+    rim_copy = pltpu.make_async_remote_copy(
+        src_ref=volts.at[:, pl.ds(span - early, early)], dst_ref=rim,
+        send_sem=sem_rim.at[0], recv_sem=sem_rim.at[1],
+        device_id={"chan": lax.rem(z + 1, zs)}, device_id_type=MESH,
+    )
+    rim_copy.start()
+    rim_copy.wait()
+    for part in (0, 1):
+        before = rim[part] * jnp.minimum(z, 1)
+        frames[0:early, part * zs : (part + 1) * zs] = before.astype(jnp.float32).astype(jnp.bfloat16)
+    for first in range(0, early, 2):
+        channelize(*range(first, min(first + 2, early)))
+    staged = stage_f32[: outs * span].reshape(spectra.shape)
+    spectra[:, :, :lead] = staged[:, :, :lead].astype(jnp.bfloat16)
 
     def own_block(source, part):
         u, v = here[part]
@@ -151,15 +179,24 @@
             for side in (1, -1):
                 give(store.at[k, core, part, v, u], device_of(part, u + side, v), send_b.at[t], sem_b.at[t])
 
+        @pl.when(t >= zs - DIRECT)
+        def _():
+            for part in (0, 1):
+                u, v = here[part]
+                give(store.at[k, core, part, v, u], device_of(part, u + 2, v), send_b.at[t], sem_c.at[t])
+
     def step_b(t, k):
         arrive(sem_b.at[t], store.at[k, core, :, 0, pl.ds(0, 2)])
-        for part in (0, 1):
-            u, v = here[part]
-            way = way_of(t, part)
-            give(
-                store.at[k, core, part, v, wrap(u - way)], device_of(part, u + way, v),
-                send_b.at[t], sem_c.at[t],
-            )
+
+        @pl.when(t < zs - DIRECT)
+        def _():
+            for part in (0, 1):
+                u, v = here[part]
+                way = way_of(t, part)
+                give(
+                    store.at[k, core, part, v, wrap(u - way)], device_of(part, u + way, v),
+                    send_b.at[t], sem_c.at[t],
+                )
 
     def give_row(t, k, part, row, way, recv):
         u, v = here[part]
@@ -173,16 +210,25 @@
         for part in (0, 1):
             give_row(t, k, part, here[part][1], way_of(t, part), sem_d.at[t])
 
+        @pl.when(t >= zs - DIRECT)
+        def _():
+            for part in (0, 1):
+                give_row(t, k, part, here[part][1], 2, sem_g.at[t])
+
     def step_f(t, k):
         for part in (0, 1):
             give_row(t, k, part, here[part][1], -way_of(t, part), sem_f.at[t])
 
     def step_d(t, k):
         arrive(sem_d.at[t], store.at[k, core, :, 0])
-        for part in (0, 1):
-            v = here[part][1]
-            way = way_of(t, part)
-            give_row(t, k, part, v - way, way, sem_g.at[t])
+
+        @pl.when(t < zs - DIRECT)
+        def _():
+            for part in (0, 1):
+                v = here[part][1]
+                way = way_of(t, part)
+                give_row(t, k, part, v - way, way, sem_g.at[t])
+
         for part in (0, 1):
             v = here[part][1]
             share_row(t, k, part, v)
@@ -229,8 +275,15 @@
             product = jnp.dot(left, block, preferred_element_type=jnp.float32)
             begin = (quarter * grid_y + second) * (2 * lanes)
             columns = pl.ds(pl.multiple_of(begin, 2 * lanes), 2 * lanes)
-            out[0, 0, :, columns] += product[:lanes]
-            out[0, 1, :, columns] += product[lanes:]
+            out[0, :, columns] += product[:lanes]
+            out[1, :, columns] += product[lanes:]
+
+    def out_copy(quarter):
+        width = 2 * grid_y * lanes
+        columns = pl.ds(pl.multiple_of(quarter * width, width), width)
+        return pltpu.make_async_copy(
+            out.at[:, :, columns], out_far.at[0, :, :, columns], sem_out.at[quarter]
+        )
 
     def iteration(it, carry):
         stage(it, step_a)
@@ -244,6 +297,10 @@
             quarter = lax.rem(late, 4)
             correlate(late - quarter, quarter)
 
+            @pl.when(late >= zs - 4)
+            def _():
+                out_copy(quarter).start()
+
         stage(it - LAGS[2], step_d)
         stage(it - LAGS[4], step_e)
         return carry
@@ -259,41 +316,47 @@
         return carry
 
     lax.fori_loop(0, zs, drain, 0)
-
-
-def exchange(volts, rim, taps):
+    for quarter in range(4):
+        out_copy(quarter).wait()
+
+
+def exchange(volts, taps):
     parts, span, zs, lanes = volts.shape
-    early = rim.shape[1]
+    tap_count = taps.shape[0]
     chips = grid_x * grid_y
-    table = dft_rows(zs, early + 1)
+    result = (2, lanes, 2 * chips * lanes)
     dma = pltpu.SemaphoreType.DMA
     return pl.pallas_call(
         functools.partial(exchange_kernel, zs),
-        out_shape=jax.ShapeDtypeStruct((1, 2, lanes, 2 * chips * lanes), jnp.float32),
-        in_specs=[pl.BlockSpec(memory_space=pltpu.VMEM)] * 4,
-        out_specs=pl.BlockSpec(memory_space=pltpu.VMEM),
+        out_shape=jax.ShapeDtypeStruct((1,) + result, jnp.float32),
+        in_specs=[pl.BlockSpec(memory_space=pl.ANY)] * 2,
+        out_specs=pl.BlockSpec(memory_space=pl.ANY),
         scratch_shapes=[
+            pltpu.VMEM(result, jnp.float32),
             pltpu.VMEM((zs, 2, 2, grid_y, grid_x, span, lanes), jnp.bfloat16),
             pltpu.VMEM((2 * lanes, 8 * span), jnp.bfloat16),
-            pltpu.VMEM((early + span, 2 * zs, lanes), jnp.bfloat16),
-            pltpu.VMEM((2 * zs * span, lanes), jnp.float32),
+            pltpu.VMEM((tap_count - 1 + span, 2 * zs, lanes), jnp.bfloat16),
+            pltpu.VMEM(((2 * zs + 1) * span, lanes), jnp.float32),
             pltpu.VMEM((zs, 2, span, lanes), jnp.bfloat16),
+            pltpu.VMEM(volts.shape, volts.dtype),
+            pltpu.VMEM(taps.shape, taps.dtype),
+            pltpu.VMEM((2, tap_count - 1, zs, lanes), volts.dtype),
+            dma((2,)),
+            dma((2,)),
+            dma((4,)),
         ]
         + [dma((zs,))] * 7
         + [dma]
         + [dma((zs,))] * 3,
         compiler_params=pltpu.CompilerParams(
-            collective_id=0, has_side_effects=True, vmem_limit_bytes=40 * 1024 * 1024
+            collective_id=0, has_side_effects=True, vmem_limit_bytes=58 * 1024 * 1024
         ),
-    )(volts, rim, taps, table)
+    )(volts, taps)
 
 
 def body(voltages, fir_taps):
-    frames = voltages.shape[1]
-    tap_count = fir_taps.shape[0]
-    rim = passed_along(voltages[:, frames - (tap_count - 1) :], "chan", 1)
-    norm_factor = 1.0 / (frames * lax.axis_size("chan"))
-    return exchange(voltages, rim, fir_taps) * norm_factor
+    norm_factor = 1.0 / (voltages.shape[1] * lax.axis_size("chan"))
+    return exchange(voltages, fir_taps) * norm_factor
 
 
 def solution(mesh):

time: 87.5 us -> 87.1 us (level)
  Pallas kernels: 75.9 us -> 82.3 us
  starting transfers between devices: 4.35 us -> 0 us
  local copies, waits for them, and re-layouts: 3.42 us -> 0 us
  other arithmetic: 2.43 us -> 4.67 us
  waiting for transfers between devices: 1.16 us -> 0 us
    pallas_call x1, Pallas kernels: 75.9 us -> 82.3 us  [exchange(): pl.pallas_call(functools.partial(exchange_kernel, zs), out_shape=jax.Shap...]
    ppermute x1 -> x0, starting transfers between devices: 4.35 us -> none  [passed_along(): return lax.ppermute(x, axis, pairs)]
    unnamed x6 -> x0, local copies, waits for them, and re-layouts: 2.62 us -> none
    mul x1, other arithmetic: 2.43 us -> 4.67 us  [body(): return exchange(voltages, fir_taps) * norm_factor]
    ppermute x1 -> x0, waiting for transfers between devices: 1.16 us -> none  [passed_along(): return lax.ppermute(x, axis, pairs)]
  transfers between devices with their start and end apart: 1 -> 0, of which waited for: 1 -> 0; matrix products, arithmetic and copies ran while one was open for 0% -> 0% of each run, Pallas kernels for 0% -> 0%
where the time goes in v3:
time: 87.1 us; the launch traced here: 87 us
  Pallas kernels  82.3 us (94%)
  other arithmetic  4.67 us (5%)
    pallas_call x1, Pallas kernels, exchange(): pl.pallas_call(functools.partial(exchange_kernel, zs), out_shape=jax.Shap...  82.3 us
    mul x1, other arithmetic, body(): return exchange(voltages, fir_taps) * norm_factor  4.67 us

profile of v3, /device:TPU:1, one launch (start us, length us, event | category | flops | bytes accessed | tf_op | source)
XLA Modules:
  0.0 87.0 jit_solution(11625449776109127051)
XLA Ops:
  0.0 82.3 %shard_map.28 = f32[1,2,128,4096]{3,2,1,0:T(8,128)} custom-call(s32[2,64,16,128]{3,2,1,0:T(8,128)} %volts_far.1, f32[4,16]{1,0:T(4,128)} %taps_far.1), custom_call_target="tpu_custom_call" | custom-call | tf_op jit(solution)/shard_map/pallas_call | solution.py:329
  82.3 4.7 %broadcast_multiply_fusion = f32[1,2,128,4096]{3,2,1,0:T(8,128)} fusion(f32[1,2,128,4096]{3,2,1,0:T(8,128)} %shard_map.28), kind=kLoop, calls=%fused_computation | loop fusion | flops 1048576 | bytes 8388608 | tf_op jit(solution)/shard_map/mul | solution.py:359

commit v4 on v3

--- a/solution.py
+++ b/solution.py
@@ -10,8 +10,7 @@
 
 
 volt_scale = 1.0 / 256.0
-LAGS = (2, 4, 6, 6, 8, 12)
-DIRECT = 2
+LAGS = (2, 4, 6, 6, 9, 14)
 grid_x = 4
 grid_y = 4
 MESH = pl.DeviceIdType.MESH
@@ -31,8 +30,8 @@
 
 
 def exchange_kernel(
-    zs, volts_far, taps_far, out_far,
-    out, store, rows, frames, stage_f32, spectra, volts, taps, rim, sem_load, sem_rim, sem_out,
+    zs, volts, taps, out,
+    store, rows, frames, stage_f32, spectra, rim, sem_rim,
     sem_a, sem_b, sem_c, sem_d, sem_f, sem_g, sem_p, send_a, send_b, send_r, send_p,
 ):
     chips = grid_x * grid_y
@@ -57,13 +56,6 @@
 
     partner = chip * 2 + 1 - core
 
-    loads = (
-        pltpu.make_async_copy(volts_far, volts, sem_load.at[0]),
-        pltpu.make_async_copy(taps_far, taps, sem_load.at[1]),
-    )
-    for copy in loads:
-        copy.start()
-
     barrier = pltpu.get_barrier_semaphore()
 
     def greet_z(step, carry):
@@ -73,14 +65,12 @@
         return carry
 
     lax.fori_loop(1, zs, greet_z, 0)
-    for du, dv in ((1, 0), (-1, 0), (2, 0), (0, 1), (0, -1), (0, 2)):
+    for du, dv in ((1, 0), (-1, 0), (0, 1), (0, -1)):
         pl.semaphore_signal(
             barrier, inc=1, device_id={"inp": device_of(0, x + du, y + dv)}, device_id_type=MESH
         )
     pl.semaphore_signal(barrier, inc=1, device_id={"inp": partner}, device_id_type=MESH)
 
-    for copy in loads:
-        copy.wait()
     for part in (0, 1):
         frames[early:, part * zs : (part + 1) * zs] = (
             volts[part].astype(jnp.float32).astype(jnp.bfloat16)
@@ -113,7 +103,7 @@
     staged = stage_f32[: outs * span].reshape(spectra.shape)
     spectra[:, :, lead:] = staged[:, :, lead:].astype(jnp.bfloat16)
     out[...] = jnp.zeros_like(out)
-    pl.semaphore_wait(barrier, zs + 6)
+    pl.semaphore_wait(barrier, zs + 4)
 
     rim_copy = pltpu.make_async_remote_copy(
         src_ref=volts.at[:, pl.ds(span - early, early)], dst_ref=rim,
@@ -172,31 +162,34 @@
     def way_of(t, part):
         return 1 - 2 * lax.rem(t + part, 2)
 
+    def give_block(t, k, part, shift):
+        u, v = here[part]
+        give(
+            store.at[k, core, part, v, wrap(u + shift)], device_of(part, u, v + way_of(t, part)),
+            send_r.at[t], sem_d.at[t],
+        )
+
     def step_a(t, k):
         arrive(sem_a.at[k], store.at[k, core, :, 0, 0])
         for part in (0, 1):
             u, v = here[part]
             for side in (1, -1):
                 give(store.at[k, core, part, v, u], device_of(part, u + side, v), send_b.at[t], sem_b.at[t])
-
-        @pl.when(t >= zs - DIRECT)
-        def _():
-            for part in (0, 1):
-                u, v = here[part]
-                give(store.at[k, core, part, v, u], device_of(part, u + 2, v), send_b.at[t], sem_c.at[t])
+        for part in (0, 1):
+            give_block(t, k, part, 0)
 
     def step_b(t, k):
         arrive(sem_b.at[t], store.at[k, core, :, 0, pl.ds(0, 2)])
-
-        @pl.when(t < zs - DIRECT)
-        def _():
+        for part in (0, 1):
+            u, v = here[part]
+            way = way_of(t, part)
+            give(
+                store.at[k, core, part, v, wrap(u - way)], device_of(part, u + way, v),
+                send_b.at[t], sem_c.at[t],
+            )
+        for shift in (1, -1):
             for part in (0, 1):
-                u, v = here[part]
-                way = way_of(t, part)
-                give(
-                    store.at[k, core, part, v, wrap(u - way)], device_of(part, u + way, v),
-                    send_b.at[t], sem_c.at[t],
-                )
+                give_block(t, k, part, shift)
 
     def give_row(t, k, part, row, way, recv):
         u, v = here[part]
@@ -208,12 +201,7 @@
     def step_c(t, k):
         arrive(sem_c.at[t], store.at[k, core, :, 0, 0])
         for part in (0, 1):
-            give_row(t, k, part, here[part][1], way_of(t, part), sem_d.at[t])
-
-        @pl.when(t >= zs - DIRECT)
-        def _():
-            for part in (0, 1):
-                give_row(t, k, part, here[part][1], 2, sem_g.at[t])
+            give_block(t, k, part, 2)
 
     def step_f(t, k):
         for part in (0, 1):
@@ -221,14 +209,10 @@
 
     def step_d(t, k):
         arrive(sem_d.at[t], store.at[k, core, :, 0])
-
-        @pl.when(t < zs - DIRECT)
-        def _():
-            for part in (0, 1):
-                v = here[part][1]
-                way = way_of(t, part)
-                give_row(t, k, part, v - way, way, sem_g.at[t])
-
+        for part in (0, 1):
+            v = here[part][1]
+            way = way_of(t, part)
+            give_row(t, k, part, v - way, way, sem_g.at[t])
         for part in (0, 1):
             v = here[part][1]
             share_row(t, k, part, v)
@@ -275,15 +259,8 @@
             product = jnp.dot(left, block, preferred_element_type=jnp.float32)
             begin = (quarter * grid_y + second) * (2 * lanes)
             columns = pl.ds(pl.multiple_of(begin, 2 * lanes), 2 * lanes)
-            out[0, :, columns] += product[:lanes]
-            out[1, :, columns] += product[lanes:]
-
-    def out_copy(quarter):
-        width = 2 * grid_y * lanes
-        columns = pl.ds(pl.multiple_of(quarter * width, width), width)
-        return pltpu.make_async_copy(
-            out.at[:, :, columns], out_far.at[0, :, :, columns], sem_out.at[quarter]
-        )
+            out[0, 0, :, columns] += product[:lanes]
+            out[0, 1, :, columns] += product[lanes:]
 
     def iteration(it, carry):
         stage(it, step_a)
@@ -297,9 +274,6 @@
             quarter = lax.rem(late, 4)
             correlate(late - quarter, quarter)
 
-            @pl.when(late >= zs - 4)
-            def _():
-                out_copy(quarter).start()
 
         stage(it - LAGS[2], step_d)
         stage(it - LAGS[4], step_e)
@@ -316,8 +290,6 @@
         return carry
 
     lax.fori_loop(0, zs, drain, 0)
-    for quarter in range(4):
-        out_copy(quarter).wait()
 
 
 def exchange(volts, taps):
@@ -329,27 +301,22 @@
     return pl.pallas_call(
         functools.partial(exchange_kernel, zs),
         out_shape=jax.ShapeDtypeStruct((1,) + result, jnp.float32),
-        in_specs=[pl.BlockSpec(memory_space=pl.ANY)] * 2,
-        out_specs=pl.BlockSpec(memory_space=pl.ANY),
+        in_specs=[pl.BlockSpec(memory_space=pltpu.VMEM)] * 2,
+        out_specs=pl.BlockSpec(memory_space=pltpu.VMEM),
         scratch_shapes=[
-            pltpu.VMEM(result, jnp.float32),
             pltpu.VMEM((zs, 2, 2, grid_y, grid_x, span, lanes), jnp.bfloat16),
             pltpu.VMEM((2 * lanes, 8 * span), jnp.bfloat16),
             pltpu.VMEM((tap_count - 1 + span, 2 * zs, lanes), jnp.bfloat16),
             pltpu.VMEM(((2 * zs + 1) * span, lanes), jnp.float32),
             pltpu.VMEM((zs, 2, span, lanes), jnp.bfloat16),
-            pltpu.VMEM(volts.shape, volts.dtype),
-            pltpu.VMEM(taps.shape, taps.dtype),
             pltpu.VMEM((2, tap_count - 1, zs, lanes), volts.dtype),
             dma((2,)),
-            dma((2,)),
-            dma((4,)),
         ]
         + [dma((zs,))] * 7
         + [dma]
         + [dma((zs,))] * 3,
         compiler_params=pltpu.CompilerParams(
-            collective_id=0, has_side_effects=True, vmem_limit_bytes=58 * 1024 * 1024
+            collective_id=0, has_side_effects=True, vmem_limit_bytes=40 * 1024 * 1024
         ),
     )(volts, taps)
 

time: 87.1 us -> 82 us (0.941)
  Pallas kernels: 82.3 us -> 77.5 us
  other arithmetic: 4.67 us -> 2.43 us
  local copies, waits for them, and re-layouts: 0 us -> 1.91 us
    pallas_call x1, Pallas kernels: 82.3 us -> 77.5 us  [exchange(): pl.pallas_call(functools.partial(exchange_kernel, zs), out_shape=jax.Shap...]
    mul x1, other arithmetic: 4.67 us -> 2.43 us  [body(): return exchange(voltages, fir_taps) * norm_factor]
    unnamed x0 -> x4, local copies, waits for them, and re-layouts: none -> 1.91 us
where the time goes in v4:
time: 82 us; the launch traced here: 81.8 us
  Pallas kernels  77.5 us (95%)
  other arithmetic  2.43 us (3%)
  local copies, waits for them, and re-layouts  1.91 us (2%)
    pallas_call x1, Pallas kernels, exchange(): pl.pallas_call(functools.partial(exchange_kernel, zs), out_shape=jax.Shap...  77.5 us
    mul x1, other arithmetic, body(): return exchange(voltages, fir_taps) * norm_factor  2.43 us
    unnamed x4, local copies, waits for them, and re-layouts  1.91 us

profile of v4, /device:TPU:1, one launch (start us, length us, event | category | flops | bytes accessed | tf_op | source)
XLA Modules:
  0.0 81.8 jit_solution(16093756334995312765)
XLA Ops:
  0.0 0.0 copy-start
  0.0 1.2 %copy-done = s32[2,64,16,128]{3,2,1,0:T(8,128)S(1)} copy-done((s32[2,64,16,128]{3,2,1,0:T(8,128)S(1)}, s32[2,64,16,128]{3,2,1,0:T(8,128)}, u32[]{:S(2)}) %copy-start) | copy-done | bytes 1048600
  1.2 0.0 copy-start.1
  1.2 0.7 copy-done.1
  1.9 77.5 %shard_map.28 = f32[1,2,128,4096]{3,2,1,0:T(8,128)S(1)} custom-call(s32[2,64,16,128]{3,2,1,0:T(8,128)S(1)} %copy-done, f32[4,16]{1,0:T(4,128)S(1)} %copy-done.1), custom_call_target="tpu_custom_call" | custom-call | tf_op jit(solution)/shard_map/pallas_call | solution.py:301
  79.4 2.4 %broadcast_multiply_fusion = f32[1,2,128,4096]{3,2,1,0:T(8,128)} fusion(f32[1,2,128,4096]{3,2,1,0:T(8,128)S(1)} %shard_map.28), kind=kLoop, calls=%fused_computation | loop fusion | flops 1048576 | bytes 8388608 | tf_op jit(solution)/shard_map/mul | solution.py:326
Async XLA Ops:
  0.0 1.2 %copy-start = (s32[2,64,16,128]{3,2,1,0:T(8,128)S(1)}, s32[2,64,16,128]{3,2,1,0:T(8,128)}, u32[]{:S(2)}) copy-start(s32[2,64,16,128]{3,2,1,0:T(8,128)} %volts.1) | copy-start | bytes 3145732
  1.2 0.7 copy-start.1

commit v5 on v4

--- a/solution.py
+++ b/solution.py
@@ -10,7 +10,7 @@
 
 
 volt_scale = 1.0 / 256.0
-LAGS = (2, 4, 6, 6, 9, 14)
+LAGS = (2, 4, 6, 6, 9, 13)
 grid_x = 4
 grid_y = 4
 MESH = pl.DeviceIdType.MESH
@@ -31,7 +31,7 @@
 
 def exchange_kernel(
     zs, volts, taps, out,
-    store, rows, frames, stage_f32, spectra, rim, sem_rim,
+    store, rows, last_rows, frames, stage_f32, spectra, rim, sem_rim,
     sem_a, sem_b, sem_c, sem_d, sem_f, sem_g, sem_p, send_a, send_b, send_r, send_p,
 ):
     chips = grid_x * grid_y
@@ -226,14 +226,14 @@
             share_row(t, k, part, v + way_of(t, part))
             share_row(t, k, part, v + 2)
 
-    def correlate(t, quarter):
-        ks = [source_of(t + step) for step in range(4)]
+    def correlate(t, count, quarter, rows):
+        ks = [source_of(t + step) for step in range(count)]
 
         @pl.when(quarter == 0)
         def _():
             for step, k in enumerate(ks):
                 arrive(sem_p.at[t + step], store.at[k, 1 - core])
-            depth = 4 * span
+            depth = count * span
             mine = []
             for part in (0, 1):
                 u, v = here[part]
@@ -262,6 +262,18 @@
             out[0, 0, :, columns] += product[:lanes]
             out[0, 1, :, columns] += product[lanes:]
 
+    def settle(t, k):
+        arrive(send_b.at[t], store.at[0, 0, :, 0, pl.ds(0, 3)])
+        arrive(send_r.at[t], store.at[0, 0, :, pl.ds(0, 3)])
+        arrive(send_p.at[t], store.at[0, 0])
+
+    def finish(t):
+        def one_quarter(quarter, carry):
+            correlate(t, 2, quarter, last_rows)
+            return carry
+
+        return one_quarter
+
     def iteration(it, carry):
         stage(it, step_a)
         stage(it - LAGS[0], step_b)
@@ -269,27 +281,27 @@
         stage(it - LAGS[3], step_f)
         late = it - LAGS[5]
 
-        @pl.when(jnp.logical_and(late >= 0, late < zs))
+        @pl.when(jnp.logical_and(late >= 0, late < zs - 4))
         def _():
             quarter = lax.rem(late, 4)
-            correlate(late - quarter, quarter)
-
+            correlate(late - quarter, 4, quarter, rows)
+
+        ending = it - (zs + LAGS[4] - 2)
+
+        @pl.when(ending >= 0)
+        def _():
+            lax.fori_loop(2 * ending, 2 * ending + 2, finish(zs - 4), 0)
 
         stage(it - LAGS[2], step_d)
         stage(it - LAGS[4], step_e)
+        stage(it - LAGS[4] - 2, settle)
         return carry
 
-    lax.fori_loop(0, zs + LAGS[5], iteration, 0)
-
+    lax.fori_loop(0, zs + LAGS[4], iteration, 0)
     arrive(send_a, spectra.at[pl.ds(0, zs - 1)])
-
-    def drain(t, carry):
-        arrive(send_b.at[t], store.at[0, 0, :, 0, pl.ds(0, 3)])
-        arrive(send_r.at[t], store.at[0, 0, :, pl.ds(0, 3)])
-        arrive(send_p.at[t], store.at[0, 0])
-        return carry
-
-    lax.fori_loop(0, zs, drain, 0)
+    lax.fori_loop(0, 4, finish(zs - 2), 0)
+    for t in (zs - 2, zs - 1):
+        settle(t, 0)
 
 
 def exchange(volts, taps):
@@ -306,6 +318,7 @@
         scratch_shapes=[
             pltpu.VMEM((zs, 2, 2, grid_y, grid_x, span, lanes), jnp.bfloat16),
             pltpu.VMEM((2 * lanes, 8 * span), jnp.bfloat16),
+            pltpu.VMEM((2 * lanes, 4 * span), jnp.bfloat16),
             pltpu.VMEM((tap_count - 1 + span, 2 * zs, lanes), jnp.bfloat16),
             pltpu.VMEM(((2 * zs + 1) * span, lanes), jnp.float32),
             pltpu.VMEM((zs, 2, span, lanes), jnp.bfloat16),

time: 82 us -> 81.7 us (level)
  no operation moved by 1% of the time
where the time goes in v5:
time: 81.7 us; the launch traced here: 81.5 us
  Pallas kernels  77.2 us (94%)
  other arithmetic  2.43 us (3%)
  local copies, waits for them, and re-layouts  1.91 us (2%)
    pallas_call x1, Pallas kernels, exchange(): pl.pallas_call(functools.partial(exchange_kernel, zs), out_shape=jax.Shap...  77.2 us
    mul x1, other arithmetic, body(): return exchange(voltages, fir_taps) * norm_factor  2.43 us
    unnamed x4, local copies, waits for them, and re-layouts  1.91 us

profile of v5, /device:TPU:1, one launch (start us, length us, event | category | flops | bytes accessed | tf_op | source)
XLA Modules:
  0.0 81.5 jit_solution(8130017422943020706)
XLA Ops:
  0.0 0.0 copy-start
  0.0 1.2 %copy-done = s32[2,64,16,128]{3,2,1,0:T(8,128)S(1)} copy-done((s32[2,64,16,128]{3,2,1,0:T(8,128)S(1)}, s32[2,64,16,128]{3,2,1,0:T(8,128)}, u32[]{:S(2)}) %copy-start) | copy-done | bytes 1048600
  1.2 0.0 copy-start.1
  1.2 0.7 copy-done.1
  1.9 77.2 %shard_map.28 = f32[1,2,128,4096]{3,2,1,0:T(8,128)S(1)} custom-call(s32[2,64,16,128]{3,2,1,0:T(8,128)S(1)} %copy-done, f32[4,16]{1,0:T(4,128)S(1)} %copy-done.1), custom_call_target="tpu_custom_call" | custom-call | tf_op jit(solution)/shard_map/pallas_call | solution.py:313
  79.1 2.4 %broadcast_multiply_fusion = f32[1,2,128,4096]{3,2,1,0:T(8,128)} fusion(f32[1,2,128,4096]{3,2,1,0:T(8,128)S(1)} %shard_map.28), kind=kLoop, calls=%fused_computation | loop fusion | flops 1048576 | bytes 8388608 | tf_op jit(solution)/shard_map/mul | solution.py:339
Async XLA Ops:
  0.0 1.2 %copy-start = (s32[2,64,16,128]{3,2,1,0:T(8,128)S(1)}, s32[2,64,16,128]{3,2,1,0:T(8,128)}, u32[]{:S(2)}) copy-start(s32[2,64,16,128]{3,2,1,0:T(8,128)} %volts.1) | copy-start | bytes 3145732
  1.2 0.7 copy-start.1

commit v6 on v5

--- a/solution.py
+++ b/solution.py
@@ -96,21 +96,22 @@
         return carry
 
     half = (span - early) // 2
-    lax.fori_loop(0, half, channelize_pair, 0, unroll=2)
+    lax.fori_loop(0, half // 2, channelize_pair, 0, unroll=5)
+    pl.semaphore_wait(barrier, zs + 4)
+
+    rim_copy = pltpu.make_async_remote_copy(
+        src_ref=volts.at[:, pl.ds(span - early, early)], dst_ref=rim,
+        send_sem=sem_rim.at[0], recv_sem=sem_rim.at[1],
+        device_id={"chan": lax.rem(z + 1, zs)}, device_id_type=MESH,
+    )
+    rim_copy.start()
+    lax.fori_loop(half // 2, half, channelize_pair, 0, unroll=5)
     if early + 2 * half < span:
         channelize(span - 1)
     lead = min(16, span // 2)
     staged = stage_f32[: outs * span].reshape(spectra.shape)
     spectra[:, :, lead:] = staged[:, :, lead:].astype(jnp.bfloat16)
     out[...] = jnp.zeros_like(out)
-    pl.semaphore_wait(barrier, zs + 4)
-
-    rim_copy = pltpu.make_async_remote_copy(
-        src_ref=volts.at[:, pl.ds(span - early, early)], dst_ref=rim,
-        send_sem=sem_rim.at[0], recv_sem=sem_rim.at[1],
-        device_id={"chan": lax.rem(z + 1, zs)}, device_id_type=MESH,
-    )
-    rim_copy.start()
     rim_copy.wait()
     for part in (0, 1):
         before = rim[part] * jnp.minimum(z, 1)

time: 81.7 us -> 81.6 us (level)
  no operation moved by 1% of the time
where the time goes in v6:
time: 81.6 us; the launch traced here: 81.4 us
  Pallas kernels  77.1 us (94%)
  other arithmetic  2.43 us (3%)
  local copies, waits for them, and re-layouts  1.91 us (2%)
    pallas_call x1, Pallas kernels, exchange(): pl.pallas_call(functools.partial(exchange_kernel, zs), out_shape=jax.Shap...  77.1 us
    mul x1, other arithmetic, body(): return exchange(voltages, fir_taps) * norm_factor  2.43 us
    unnamed x4, local copies, waits for them, and re-layouts  1.91 us

profile of v6, /device:TPU:1, one launch (start us, length us, event | category | flops | bytes accessed | tf_op | source)
XLA Modules:
  0.0 81.4 jit_solution(3801289124571475889)
XLA Ops:
  0.0 0.0 copy-start
  0.0 1.2 %copy-done = s32[2,64,16,128]{3,2,1,0:T(8,128)S(1)} copy-done((s32[2,64,16,128]{3,2,1,0:T(8,128)S(1)}, s32[2,64,16,128]{3,2,1,0:T(8,128)}, u32[]{:S(2)}) %copy-start) | copy-done | bytes 1048600
  1.2 0.0 copy-start.1
  1.2 0.7 copy-done.1
  1.9 77.1 %shard_map.28 = f32[1,2,128,4096]{3,2,1,0:T(8,128)S(1)} custom-call(s32[2,64,16,128]{3,2,1,0:T(8,128)S(1)} %copy-done, f32[4,16]{1,0:T(4,128)S(1)} %copy-done.1), custom_call_target="tpu_custom_call" | custom-call | tf_op jit(solution)/shard_map/pallas_call | solution.py:314
  79.0 2.4 %broadcast_multiply_fusion = f32[1,2,128,4096]{3,2,1,0:T(8,128)} fusion(f32[1,2,128,4096]{3,2,1,0:T(8,128)S(1)} %shard_map.28), kind=kLoop, calls=%fused_computation | loop fusion | flops 1048576 | bytes 8388608 | tf_op jit(solution)/shard_map/mul | solution.py:340
Async XLA Ops:
  0.0 1.2 %copy-start = (s32[2,64,16,128]{3,2,1,0:T(8,128)S(1)}, s32[2,64,16,128]{3,2,1,0:T(8,128)}, u32[]{:S(2)}) copy-start(s32[2,64,16,128]{3,2,1,0:T(8,128)} %volts.1) | copy-start | bytes 3145732
  1.2 0.7 copy-start.1
